TPU v7x, 32 devices: a whole 2x2x4 slice. The times are simulated.
32 devices in a mesh: sec: 4 (over x, core), sub: 8 (over z, y).
Axes of the slice: x: 2, y: 2, z: 4, core: 2. Of those that a mesh axis runs over, the one named last changes fastest.
Arguments:
- schur: bfloat16 [8, 1024, 1024], P('sub', 'sec'), may hold values from -0.1875 to 0.1875
- neumann: bfloat16 [8, 1024, 1024], P('sub', 'sec'), may hold values from -0.1875 to 0.1875
- constraint_weights: bfloat16 [8, 1024, 128], P('sub', 'sec'), may hold values from -0.1875 to 0.1875
- coarse_inverse: bfloat16 [8, 768, 768], P('sub', 'sec'), may hold values from -0.21875 to 0.21875
- solution: bfloat16 [8, 1024, 128], P('sub', 'sec'), may hold values from -6 to 6
- load: bfloat16 [8, 1024, 128], P('sub', 'sec'), may hold values from -6 to 6
- neighbours: int32 [8, 4], P('sub'), may hold values from 0 to 7, as said below
- face_index: int32 [8, 1024], P('sub', 'sec'), may hold values from 0 to 255, as said below
- coarse_dof: int32 [8, 128], P('sub'), may hold values from 0 to 6143, as said below
Outputs:
- precond: bfloat16 [8, 1024, 128], P('sub', 'sec')
- image: bfloat16 [8, 1024, 128], P('sub', 'sec')
Inputs may be any that keep to these rules, and one draw needn't show every extreme that they name: `neighbours`: the subdomain glued to face f of subdomain i is another subdomain whose column c // 1 is the column i // 1 of i or the one before or after it, cyclically over 8 columns. `face_index`: for each subdomain and face, the entries of the face's 256 unknowns are a permutation of 0 to 255. `coarse_dof`: constraint k of subdomain i maps to an unknown of the cluster of column i // 1 or of the column before or after it, cyclically. Each cluster has 64 coarse unknowns that are used, and each used unknown is the unknown of exactly two constraints.
All inputs are finite; a program needn't handle non-finite values.
Results may differ from a plain program's by a relative error of at most 0.0058.
Values may be sent and summed in bfloat16 or wider, within the bound.
No kernel may reach another device: no remote copies, remote signals or barrier semaphores. Data moves between devices by JAX's collectives and lax.ppermute only.
A program may use at most 64 MiB of HBM per device.

v0:
```python
import jax
import jax.numpy as jnp
from jax import lax
from jax.sharding import PartitionSpec as P

F32 = jnp.float32
BF16 = jnp.bfloat16
KINDS = ("A2", "B2", "A3", "B3")


def partner(kind, i, count):
    forward = {
        "A": i % 2 == 0,
        "B": i % 2 == 1,
        "A2": i % 4 < 2,
        "B2": i % 4 >= 2,
        "A3": i % 2 == 0,
        "B3": i % 2 == 1,
    }[kind]
    step = {"2": 2, "3": 3}.get(kind[-1], 1)
    return (i + step if forward else i - step) % count


def swap_columns(array, kind):
    count = lax.axis_size("sub")
    return lax.ppermute(array, "sub", [(i, partner(kind, i, count)) for i in range(count)])


def swap_by_section(array, kinds):
    sections, count = (lax.axis_size("sec"), lax.axis_size("sub"))
    moves = [
        (s * count + i, s * count + partner(kinds[s % len(kinds)], i, count))
        for s in range(sections)
        for i in range(count)
    ]
    return lax.ppermute(array, ("sec", "sub"), moves)


def swap_cores(array):
    return lax.ppermute(array, "sec", [(i, i ^ 1) for i in range(lax.axis_size("sec"))])


def dot(a, b):
    return jnp.dot(a, b, preferred_element_type=F32)


def encode_dof(dof, column, count, coarse_len):
    near = (dof // coarse_len - column + 1) % count
    slot = dof % coarse_len
    parts = -(-coarse_len // 128)
    rows = jnp.stack([near * parts + slot // 128, slot % 128]).astype(BF16)
    return jnp.pad(rows, ((0, 14), (0, 0)))


def decode_dof(rows, offset, coarse_len):
    parts = -(-coarse_len // 128)
    whole = rows[:2].astype(F32).astype(jnp.int32)
    cluster = offset + 1 + whole[0] // parts
    return (cluster, whole[0] % parts * 128 + whole[1])


def local(
    schur,
    neumann,
    constraint_weights,
    coarse_inverse,
    solution,
    load,
    neighbours,
    face_index,
    coarse_dof,
):
    s_rows, n_rows, weights = (schur[0], neumann[0], constraint_weights[0])
    c_rows = coarse_inverse[0]
    face_len, cons = weights.shape
    coarse_part, coarse_len = c_rows.shape
    used = cons // 2
    column, section = (lax.axis_index("sub"), lax.axis_index("sec"))
    count = lax.axis_size("sub")
    core = section % 2
    even = column % 2 == 0
    off1 = jnp.where(even, 1, -1)
    off2 = jnp.where(column % 4 < 2, 2, -2)
    off3 = jnp.where(even, 3, -3)
    own_code = encode_dof(coarse_dof[0], column, count, coarse_len)
    far_code = swap_by_section(own_code, KINDS)
    first = jnp.concatenate([weights, own_code])
    near_b = swap_columns(first, "B")
    near_a = swap_columns(first, "A")
    iterate = lax.all_gather(solution[0], "sec", axis=0, tiled=True)
    residual = load[0].astype(F32) - dot(s_rows, iterate)
    residual_half = residual.astype(BF16)
    res_b = swap_columns(residual_half, "B")
    res_a = swap_columns(residual_half, "A")
    nbr = neighbours[0, section]
    want_a = (nbr - column - off1) % count == 0
    positions = lax.broadcasted_iota(jnp.int32, (face_len, face_len), 1)
    selector = (face_index[0][:, None] == positions).astype(BF16)
    dec = lambda rows, off: decode_dof(rows, off, coarse_len)
    parts3 = [dec(own_code, 0), dec(near_a[face_len:], off1), dec(near_b[face_len:], -off1)]
    clus3 = jnp.concatenate([p[0] for p in parts3])
    slot3 = jnp.concatenate([p[1] for p in parts3])
    key3 = jnp.where(clus3 == 2, slot3, -1)
    less = (key3[None, :] >= 0) & (key3[None, :] < key3[:, None])
    rank3 = jnp.where(key3 >= 0, jnp.sum(less.astype(jnp.int32), axis=1) // 2, -1)
    by_rank = (lax.broadcasted_iota(jnp.int32, (used, 3 * cons), 0) == rank3[None, :]).astype(BF16)
    by_slot = (key3[:, None] == lax.broadcasted_iota(jnp.int32, (3 * cons, coarse_len), 1)).astype(
        BF16
    )
    pick_used = dot(by_rank, by_slot).astype(BF16)
    used_cols = lax.dot_general(
        c_rows, pick_used, (((1,), (1,)), ((), ())), preferred_element_type=F32
    ).astype(BF16)
    pick_rows = lax.dynamic_slice_in_dim(pick_used, section * coarse_part, coarse_part, axis=1)
    used_part = (0.25 * dot(pick_rows, used_cols)).astype(BF16)
    used_part = jnp.pad(used_part, ((0, 0), (0, cons - used)))
    matched = jnp.where(want_a, res_a, res_b)
    assembled = (residual + dot(selector, matched)).astype(BF16)
    values_part = lax.dot_general(
        weights, assembled, (((0,), (0,)), ((), ())), preferred_element_type=F32
    ).astype(BF16)
    packed = jnp.concatenate([assembled, values_part, used_part, far_code])
    around = lax.all_gather(packed, "sec", axis=0)
    assembled_all = around[:, :face_len].reshape(-1, around.shape[2])
    values = jnp.sum(around[:, face_len : face_len + cons].astype(F32), axis=0).astype(BF16)
    at = face_len + cons
    used_block = jnp.sum(around[:, at : at + used].astype(F32), axis=0).astype(BF16)
    far_codes = around[:, at + used :]
    correction = dot(n_rows, assembled_all)
    coarse_load = jnp.concatenate([values, used_block])
    out = jnp.concatenate([correction.astype(BF16), coarse_load])
    far2_mine = swap_by_section(coarse_load, KINDS[:2])
    far3_mine = swap_by_section(values, KINDS[2:])
    cor_b = swap_columns(out, "B")
    cor_a = swap_columns(out, "A")
    far_mine = jnp.concatenate([far2_mine, far3_mine])
    far_other = swap_cores(far_mine)
    sign = jnp.where(core == 0, 1, -1)
    c0 = lambda x, y: jnp.where(core == 0, x, y)
    window = parts3 + [
        dec(c0(far_codes[0], far_codes[1]), sign * off2),
        dec(c0(far_codes[1], far_codes[0]), -sign * off2),
        dec(c0(far_codes[2], far_codes[3]), sign * off3),
        dec(c0(far_codes[3], far_codes[2]), -sign * off3),
    ]
    clus = jnp.concatenate([p[0] for p in window])
    slot = jnp.concatenate([p[1] for p in window])
    inside = (clus >= 0) & (clus < 5)
    same_less = (clus[None, :] == clus[:, None]) & (slot[None, :] < slot[:, None])
    rank = jnp.sum(same_less.astype(jnp.int32), axis=1) // 2
    order = [0, off1, -off1, sign * off2, -sign * off2]
    place = sum((jnp.where(clus == 2 + order[m], m, 0) for m in range(1, 5)))
    code = jnp.where(inside, place * used + rank, -1)
    unknowns = 5 * used
    spread = (lax.broadcasted_iota(jnp.int32, (unknowns, 7 * cons), 0) == code[None, :]).astype(
        BF16
    )
    nbr_code = jnp.where(want_a, code[cons : 2 * cons], code[2 * cons : 3 * cons])
    pair_code = jnp.concatenate([code[:cons], nbr_code])
    gather = (
        pair_code[:, None] == lax.broadcasted_iota(jnp.int32, (2 * cons, unknowns), 1)
    ).astype(BF16)
    weights_nbr = jnp.where(want_a, near_a[:face_len], near_b[:face_len])
    weights_pair = jnp.concatenate([weights, dot(selector, weights_nbr).astype(BF16)], axis=1)
    far = coarse_load.shape[0]
    values_near = jnp.concatenate(
        [
            values,
            cor_a[face_len : face_len + cons],
            cor_b[face_len : face_len + cons],
            far_mine[:cons],
            far_other[:cons],
            far_mine[far:],
            far_other[far:],
        ]
    )
    blocks = jnp.stack(
        [
            used_block,
            cor_a[face_len + cons :],
            cor_b[face_len + cons :],
            far_mine[cons:far],
            far_other[cons:far],
        ]
    )[:, :, :used]
    rhs = dot(spread, values_near).astype(BF16).reshape(5, used, -1)
    coarse = jnp.einsum("quv,qvc->quc", blocks, rhs, preferred_element_type=F32).astype(BF16)
    picked = dot(gather, coarse.reshape(unknowns, -1)).astype(BF16)
    facing = dot(selector, jnp.where(want_a, cor_a[:face_len], cor_b[:face_len]))
    precond = (0.5 * (correction + facing + dot(weights_pair, picked))).astype(BF16)
    precond_all = lax.all_gather(precond, "sec", axis=0, tiled=True)
    image = dot(s_rows, precond_all).astype(BF16)
    return (precond[None], image[None])


def solution(mesh):
    placed = (
        P("sub", "sec", None),
        P("sub", "sec", None),
        P("sub", "sec", None),
        P("sub", "sec", None),
        P("sub", "sec", None),
        P("sub", "sec", None),
        P("sub", None),
        P("sub", "sec"),
        P("sub", None),
    )
    return jax.shard_map(
        local,
        mesh=mesh,
        in_specs=placed,
        out_specs=(P("sub", "sec", None), P("sub", "sec", None)),
        check_vma=False,
    )
```

profile of v0, /device:TPU:0, one launch (start us, length us, event | category | flops | bytes accessed | tf_op | source)
XLA Modules:
  0.0 52.0 jit_solution(424004631807403690)
XLA Ops:
  0.6 0.0 copy-start
  0.6 0.0 copy-start.5
  0.7 0.7 %fusion.84 = (bf16[1,128]{1,0:T(2,128)(2,1)S(1)}, s32[1,128]{1,0:T(1,128)S(1)}) fusion(s32[1,128]{1,0:T(1,128)} %param.17, s32[]{:T(128)S(6)} %axis_index.25), kind=kLoop, calls=%fused_computation.216 | loop fusion | flops 5504 | bytes 1284 | tf_op jit(solution)/shard_map/convert.3
  1.4 3.1 %collective-permute-start.4 = (bf16[16,128]{1,0:T(8,128)(2,1)S(1)}, bf16[16,128]{1,0:T(8,128)(2,1)S(1)}, u32[]{:S(2)}, u32[]{:S(2)}) collective-permute-start(bf16[16,128]{1,0:T(8,128)(2,1)S(1)} %pad.8), channel_id=1, source_target_pairs={{0,2},{1,3},{2,0},{3,1},{4,6},{5,7},{6,4},{7,5},{8,14},{9,15},{10,... | collective-permute-start | bytes 12296 | tf_op jit(solution)/shard_map/ppermute | solution.py:36
  4.6 0.8 %pad_maximum_fusion.2 = bf16[272,128]{1,0:T(8,128)(2,1)S(1)} fusion(bf16[16,128]{1,0:T(8,128)(2,1)S(1)} %pad.8, bf16[256,128]{1,0:T(8,128)(2,1)} %bitcast.261), kind=kLoop, calls=%fused_computation.54 | loop fusion | flops 139264 | bytes 139264 | tf_op jit(solution)/shard_map/concatenate | solution.py:87
  5.4 3.4 %collective-permute-start.3 = (bf16[272,128]{1,0:T(8,128)(2,1)S(1)}, bf16[272,128]{1,0:T(8,128)(2,1)S(1)}, u32[]{:S(2)}, u32[]{:S(2)}) collective-permute-start(bf16[272,128]{1,0:T(8,128)(2,1)S(1)} %pad_maximum_fusion.2), channel_id=1, source_target_pairs={{0,7},{1,2},{2,1},{3,4},{4,3},{5,6},{6,5},{7,0},{8,15},{9,10},{10,... | collective-permute-start | bytes 208904 | tf_op jit(solution)/shard_map/ppermute | solution.py:26
  8.8 0.0 collective-permute-start.2
  8.8 6.5 %all-gather = bf16[1,1024,128]{2,1,0:T(8,128)(2,1)S(1)} all-gather(bf16[1,256,128]{2,1,0:T(8,128)(2,1)} %param.13), channel_id=2, replica_groups=mesh['sec'=4,'sub'=8] {'sec'}, dimensions={1}, use_global_device_ids=true | all-gather | bytes 327680 | tf_op jit(solution)/shard_map/all_gather | solution.py:90
  15.3 0.0 copy-done
  15.3 0.0 copy-done.5
  15.3 0.0 copy-start.7
  15.4 0.0 copy-start.6
  15.4 0.0 copy-start.3
  15.4 0.3 fusion.95
  15.7 2.6 %collective-permute-start.1 = (bf16[256,128]{1,0:T(8,128)(2,1)S(1)}, bf16[256,128]{1,0:T(8,128)(2,1)S(1)}, u32[]{:S(2)}, u32[]{:S(2)}) collective-permute-start(bf16[256,128]{1,0:T(8,128)(2,1)S(1)} %get-tuple-element.63), channel_id=1, source_target_pairs={{0,7},{1,2},{2,1},{3,4},{4,3},{5,6},{6,5},{7,0},{8,15},{9,10},{10,... | collective-permute-start | bytes 196616 | tf_op jit(solution)/shard_map/ppermute | solution.py:26
  18.2 0.5 %collective-permute-start = (bf16[256,128]{1,0:T(8,128)(2,1)S(1)}, bf16[256,128]{1,0:T(8,128)(2,1)S(1)}, u32[]{:S(2)}, u32[]{:S(2)}) collective-permute-start(bf16[256,128]{1,0:T(8,128)(2,1)S(1)} %get-tuple-element.63), channel_id=1, source_target_pairs={{0,1},{1,0},{2,3},{3,2},{4,5},{5,4},{6,7},{7,6},{8,9},{9,8},{10,11... | collective-permute-start | bytes 196616 | tf_op jit(solution)/shard_map/ppermute | solution.py:26
  18.9 0.0 copy-done.7
  18.9 0.6 %constant_dynamic-slice_fusion = s32[1,1]{1,0:T(1,128)} fusion(s32[1,4]{1,0:T(1,128)S(1)} %copy-done.7, s32[]{:T(128)S(6)} %select_n.297), kind=kLoop, calls=%fused_computation.209 | loop fusion | bytes 12 | tf_op jit(solution)/shard_map/dynamic_slice | solution.py:95
  20.1 0.0 copy-start.2
  20.2 2.7 %collective-permute-done.1 = bf16[256,128]{1,0:T(8,128)(2,1)S(1)} collective-permute-done((bf16[256,128]{1,0:T(8,128)(2,1)S(1)}, bf16[256,128]{1,0:T(8,128)(2,1)S(1)}, u32[]{:S(2)}, u32[]{:S(2)}) %collective-permute-start.1) | collective-permute-done | bytes 65568 | tf_op jit(solution)/shard_map/ppermute | solution.py:26
  22.9 0.8 %collective-permute-done = bf16[256,128]{1,0:T(8,128)(2,1)S(1)} collective-permute-done((bf16[256,128]{1,0:T(8,128)(2,1)S(1)}, bf16[256,128]{1,0:T(8,128)(2,1)S(1)}, u32[]{:S(2)}, u32[]{:S(2)}) %collective-permute-start) | collective-permute-done | bytes 65568 | tf_op jit(solution)/shard_map/ppermute | solution.py:26
  23.7 0.0 copy-done.6
  23.7 0.2 fusion.7
  24.0 0.0 copy-done.3
  24.0 0.2 fusion.10
  24.2 0.0 collective-permute-done.3
  24.2 0.0 collective-permute-done.2
  24.4 0.2 convert_reduce_fusion.1
  24.7 0.4 fusion.2
  25.1 0.0 copy-done.2
  25.1 0.4 fusion.11
  25.5 0.0 collective-permute-done.4
  25.5 6.4 %all-gather.1 = bf16[1856,128]{1,0:T(8,128)(2,1)S(1)} all-gather(bf16[464,128]{1,0:T(8,128)(2,1)S(1)} %fusion.31), channel_id=3, replica_groups=mesh['sec'=4,'sub'=8] {'sec'}, dimensions={0}, use_global_device_ids=true | all-gather | bytes 593920 | tf_op jit(solution)/shard_map/all_gather | solution.py:123
  31.9 0.0 copy-start.1
  32.0 1.0 %collective-permute-start.8 = (bf16[128,128]{1,0:T(8,128)(2,1)S(1)}, bf16[128,128]{1,0:T(8,128)(2,1)S(1)}, u32[]{:S(2)}, u32[]{:S(2)}) collective-permute-start(bf16[128,128]{1,0:T(8,128)(2,1)S(1)} %slice_reduce_fusion), channel_id=1, source_target_pairs={{0,3},{1,6},{2,5},{3,0},{4,7},{5,2},{6,1},{7,4},{8,13},{9,12},{10,... | collective-permute-start | bytes 98312 | tf_op jit(solution)/shard_map/ppermute | solution.py:36
  33.0 0.0 copy-done.1
  33.0 0.3 fusion.96
  33.3 2.7 %collective-permute-start.6 = (bf16[448,128]{1,0:T(8,128)(2,1)S(1)}, bf16[448,128]{1,0:T(8,128)(2,1)S(1)}, u32[]{:S(2)}, u32[]{:S(2)}) collective-permute-start(bf16[448,128]{1,0:T(8,128)(2,1)S(1)} %pad_maximum_fusion), channel_id=1, source_target_pairs={{0,7},{1,2},{2,1},{3,4},{4,3},{5,6},{6,5},{7,0},{8,15},{9,10},{10,... | collective-permute-start | bytes 344072 | tf_op jit(solution)/shard_map/ppermute | solution.py:26
  36.0 0.0 collective-permute-start.5
  36.1 0.7 %convert_reduce_fusion = s32[896]{0:T(1024)S(1)} fusion(s32[896]{0:T(1024)S(1)} %get-tuple-element.46, s32[896]{0:T(1024)S(1)} %get-tuple-element.45), kind=kLoop, calls=%fused_computation | loop fusion | flops 4013184 | bytes 10752 | tf_op jit(solution)/shard_map/reduce_sum | solution.py:150
  36.9 1.8 %collective-permute-start.7 = (bf16[192,128]{1,0:T(8,128)(2,1)S(1)}, bf16[192,128]{1,0:T(8,128)(2,1)S(1)}, u32[]{:S(2)}, u32[]{:S(2)}) collective-permute-start(bf16[192,128]{1,0:T(8,128)(2,1)S(1)} %pad_maximum_fusion.3), channel_id=1, source_target_pairs={{0,2},{1,3},{2,0},{3,1},{4,6},{5,7},{6,4},{7,5},{8,14},{9,15},{10,... | collective-permute-start | bytes 147464 | tf_op jit(solution)/shard_map/ppermute | solution.py:36
  38.6 0.2 convolution_convert_fusion.3
  38.9 0.0 collective-permute-done.8
  38.9 2.1 %collective-permute-done.7 = bf16[192,128]{1,0:T(8,128)(2,1)S(1)} collective-permute-done((bf16[192,128]{1,0:T(8,128)(2,1)S(1)}, bf16[192,128]{1,0:T(8,128)(2,1)S(1)}, u32[]{:S(2)}, u32[]{:S(2)}) %collective-permute-start.7) | collective-permute-done | bytes 49184 | tf_op jit(solution)/shard_map/ppermute | solution.py:36
  41.0 1.6 %collective-permute-start.9 = (bf16[320,128]{1,0:T(8,128)(2,1)S(1)}, bf16[320,128]{1,0:T(8,128)(2,1)S(1)}, u32[]{:S(2)}, u32[]{:S(2)}) collective-permute-start(bf16[320,128]{1,0:T(8,128)(2,1)S(1)} %pad_maximum_fusion.1), channel_id=1, source_target_pairs={{0,8},{8,0},{16,24},{24,16},{1,9},{9,1},{17,25},{25,17},{2,10},{10... | collective-permute-start | bytes 245768 | tf_op jit(solution)/shard_map/ppermute | solution.py:40
  42.6 1.2 %collective-permute-done.5 = bf16[448,128]{1,0:T(8,128)(2,1)S(1)} collective-permute-done((bf16[448,128]{1,0:T(8,128)(2,1)S(1)}, bf16[448,128]{1,0:T(8,128)(2,1)S(1)}, u32[]{:S(2)}, u32[]{:S(2)}) %collective-permute-start.5) | collective-permute-done | bytes 114720 | tf_op jit(solution)/shard_map/ppermute | solution.py:26
  43.8 0.0 collective-permute-done.6
  43.9 0.0 collective-permute-done.9
  43.9 0.3 fusion.5
  44.3 0.1 convolution_convert_fusion
  44.4 0.5 fusion.9
  44.9 0.2 fusion.6
  45.1 0.0 copy-start.4
  45.1 5.8 %all_gather.15 = bf16[1024,128]{1,0:T(8,128)(2,1)S(1)} all-gather(bf16[256,128]{1,0:T(8,128)(2,1)S(1)} %fusion.6), channel_id=1, replica_groups=mesh['sec'=4,'sub'=8] {'sec'}, dimensions={0}, use_global_device_ids=true | all-gather | bytes 327680 | tf_op jit(solution)/shard_map/all_gather | solution.py:191
  50.9 0.3 fusion.8
  51.2 0.0 copy-done.4
  51.3 0.7 %copy.14 = bf16[1,256,128]{2,1,0:T(8,128)(2,1)} copy(bf16[1,256,128]{1,2,0:T(8,128)(2,1)S(1)} %fusion.8) | data formatting | bytes 131072
  (48 shorter events, 0.6 us)
Async XLA Ops:
  0.6 14.7 %copy-start = (bf16[1,256,1024]{2,1,0:T(8,128)(2,1)S(1)}, bf16[1,256,1024]{2,1,0:T(8,128)(2,1)}, u32[]{:S(2)}) copy-start(bf16[1,256,1024]{2,1,0:T(8,128)(2,1)} %param.9) | copy-start | bytes 1572868
  0.6 14.7 %copy-start.5 = (bf16[1,256,128]{2,1,0:T(8,128)(2,1)S(1)}, bf16[1,256,128]{2,1,0:T(8,128)(2,1)}, u32[]{:S(2)}) copy-start(bf16[1,256,128]{2,1,0:T(8,128)(2,1)} %param.14) | copy-start | bytes 196612
  1.4 24.0 %collective-permute-start.4 = (bf16[16,128]{1,0:T(8,128)(2,1)S(1)}, bf16[16,128]{1,0:T(8,128)(2,1)S(1)}, u32[]{:S(2)}, u32[]{:S(2)}) collective-permute-start(bf16[16,128]{1,0:T(8,128)(2,1)S(1)} %pad.8), channel_id=1, source_target_pairs={{0,2},{1,3},{2,0},{3,1},{4,6},{5,7},{6,4},{7,5},{8,14},{9,15},{10,... | collective-permute-start | bytes 12296 | tf_op jit(solution)/shard_map/ppermute | solution.py:36
  5.4 18.8 %collective-permute-start.3 = (bf16[272,128]{1,0:T(8,128)(2,1)S(1)}, bf16[272,128]{1,0:T(8,128)(2,1)S(1)}, u32[]{:S(2)}, u32[]{:S(2)}) collective-permute-start(bf16[272,128]{1,0:T(8,128)(2,1)S(1)} %pad_maximum_fusion.2), channel_id=1, source_target_pairs={{0,7},{1,2},{2,1},{3,4},{4,3},{5,6},{6,5},{7,0},{8,15},{9,10},{10,... | collective-permute-start | bytes 208904 | tf_op jit(solution)/shard_map/ppermute | solution.py:26
  8.8 15.4 %collective-permute-start.2 = (bf16[272,128]{1,0:T(8,128)(2,1)S(1)}, bf16[272,128]{1,0:T(8,128)(2,1)S(1)}, u32[]{:S(2)}, u32[]{:S(2)}) collective-permute-start(bf16[272,128]{1,0:T(8,128)(2,1)S(1)} %pad_maximum_fusion.2), channel_id=1, source_target_pairs={{0,1},{1,0},{2,3},{3,2},{4,5},{5,4},{6,7},{7,6},{8,9},{9,8},{10,11... | collective-permute-start | bytes 208904 | tf_op jit(solution)/shard_map/ppermute | solution.py:26
  15.3 3.5 %copy-start.7 = (s32[1,4]{1,0:T(1,128)S(1)}, s32[1,4]{1,0:T(1,128)}, u32[]{:S(2)}) copy-start(s32[1,4]{1,0:T(1,128)} %param.15) | copy-start | bytes 52
  15.4 8.4 %copy-start.6 = (s32[1,256]{1,0:T(1,128)S(1)}, s32[1,256]{1,0:T(1,128)}, u32[]{:S(2)}) copy-start(s32[1,256]{1,0:T(1,128)} %param.16) | copy-start | bytes 3076
  15.4 8.6 %copy-start.3 = (bf16[1,256,128]{2,1,0:T(8,128)(2,1)S(1)}, bf16[1,256,128]{2,1,0:T(8,128)(2,1)}, u32[]{:S(2)}) copy-start(bf16[1,256,128]{2,1,0:T(8,128)(2,1)} %param.11) | copy-start | bytes 196612
  15.7 7.2 %collective-permute-start.1 = (bf16[256,128]{1,0:T(8,128)(2,1)S(1)}, bf16[256,128]{1,0:T(8,128)(2,1)S(1)}, u32[]{:S(2)}, u32[]{:S(2)}) collective-permute-start(bf16[256,128]{1,0:T(8,128)(2,1)S(1)} %get-tuple-element.63), channel_id=1, source_target_pairs={{0,7},{1,2},{2,1},{3,4},{4,3},{5,6},{6,5},{7,0},{8,15},{9,10},{10,... | collective-permute-start | bytes 196616 | tf_op jit(solution)/shard_map/ppermute | solution.py:26
  18.2 5.5 %collective-permute-start = (bf16[256,128]{1,0:T(8,128)(2,1)S(1)}, bf16[256,128]{1,0:T(8,128)(2,1)S(1)}, u32[]{:S(2)}, u32[]{:S(2)}) collective-permute-start(bf16[256,128]{1,0:T(8,128)(2,1)S(1)} %get-tuple-element.63), channel_id=1, source_target_pairs={{0,1},{1,0},{2,3},{3,2},{4,5},{5,4},{6,7},{7,6},{8,9},{9,8},{10,11... | collective-permute-start | bytes 196616 | tf_op jit(solution)/shard_map/ppermute | solution.py:26
  20.1 4.9 %copy-start.2 = (bf16[1,192,768]{2,1,0:T(8,128)(2,1)S(1)}, bf16[1,192,768]{2,1,0:T(8,128)(2,1)}, u32[]{:S(2)}) copy-start(bf16[1,192,768]{2,1,0:T(8,128)(2,1)} %param.12) | copy-start | bytes 884740
  31.9 1.1 %copy-start.1 = (bf16[1,256,1024]{2,1,0:T(8,128)(2,1)S(1)}, bf16[1,256,1024]{2,1,0:T(8,128)(2,1)}, u32[]{:S(2)}) copy-start(bf16[1,256,1024]{2,1,0:T(8,128)(2,1)} %param.10) | copy-start | bytes 1572868
  32.0 7.0 %collective-permute-start.8 = (bf16[128,128]{1,0:T(8,128)(2,1)S(1)}, bf16[128,128]{1,0:T(8,128)(2,1)S(1)}, u32[]{:S(2)}, u32[]{:S(2)}) collective-permute-start(bf16[128,128]{1,0:T(8,128)(2,1)S(1)} %slice_reduce_fusion), channel_id=1, source_target_pairs={{0,3},{1,6},{2,5},{3,0},{4,7},{5,2},{6,1},{7,4},{8,13},{9,12},{10,... | collective-permute-start | bytes 98312 | tf_op jit(solution)/shard_map/ppermute | solution.py:36
  33.3 10.5 %collective-permute-start.6 = (bf16[448,128]{1,0:T(8,128)(2,1)S(1)}, bf16[448,128]{1,0:T(8,128)(2,1)S(1)}, u32[]{:S(2)}, u32[]{:S(2)}) collective-permute-start(bf16[448,128]{1,0:T(8,128)(2,1)S(1)} %pad_maximum_fusion), channel_id=1, source_target_pairs={{0,7},{1,2},{2,1},{3,4},{4,3},{5,6},{6,5},{7,0},{8,15},{9,10},{10,... | collective-permute-start | bytes 344072 | tf_op jit(solution)/shard_map/ppermute | solution.py:26
  36.0 7.8 %collective-permute-start.5 = (bf16[448,128]{1,0:T(8,128)(2,1)S(1)}, bf16[448,128]{1,0:T(8,128)(2,1)S(1)}, u32[]{:S(2)}, u32[]{:S(2)}) collective-permute-start(bf16[448,128]{1,0:T(8,128)(2,1)S(1)} %pad_maximum_fusion), channel_id=1, source_target_pairs={{0,1},{1,0},{2,3},{3,2},{4,5},{5,4},{6,7},{7,6},{8,9},{9,8},{10,11... | collective-permute-start | bytes 344072 | tf_op jit(solution)/shard_map/ppermute | solution.py:26
  36.9 4.2 %collective-permute-start.7 = (bf16[192,128]{1,0:T(8,128)(2,1)S(1)}, bf16[192,128]{1,0:T(8,128)(2,1)S(1)}, u32[]{:S(2)}, u32[]{:S(2)}) collective-permute-start(bf16[192,128]{1,0:T(8,128)(2,1)S(1)} %pad_maximum_fusion.3), channel_id=1, source_target_pairs={{0,2},{1,3},{2,0},{3,1},{4,6},{5,7},{6,4},{7,5},{8,14},{9,15},{10,... | collective-permute-start | bytes 147464 | tf_op jit(solution)/shard_map/ppermute | solution.py:36
  41.0 2.8 %collective-permute-start.9 = (bf16[320,128]{1,0:T(8,128)(2,1)S(1)}, bf16[320,128]{1,0:T(8,128)(2,1)S(1)}, u32[]{:S(2)}, u32[]{:S(2)}) collective-permute-start(bf16[320,128]{1,0:T(8,128)(2,1)S(1)} %pad_maximum_fusion.1), channel_id=1, source_target_pairs={{0,8},{8,0},{16,24},{24,16},{1,9},{9,1},{17,25},{25,17},{2,10},{10... | collective-permute-start | bytes 245768 | tf_op jit(solution)/shard_map/ppermute | solution.py:40
  45.1 6.1 %copy-start.4 = (bf16[256,128]{1,0:T(8,128)(2,1)}, bf16[256,128]{1,0:T(8,128)(2,1)S(1)}, u32[]{:S(2)}) copy-start(bf16[256,128]{1,0:T(8,128)(2,1)S(1)} %fusion.6) | copy-start | bytes 196612
where the time goes:
time: 52.2 us; the launch traced here: 52 us
  blocking collectives  18.6 us (36%)
  starting transfers between devices  16.7 us (32%)
  waiting for transfers between devices  6.86 us (13%)
  matrix products  3.55 us (7%)
  other arithmetic  2.93 us (6%)
  between operations  1.77 us (3%)
  local copies, waits for them, and re-layouts  1.5 us (3%)
    ppermute x6, starting transfers between devices, swap_columns(): lax.ppermute(array, 'sub', [(i, partner(kind, i, count)) for i in range(c...  9.27 us
    all_gather x1, blocking collectives, local(): iterate = lax.all_gather(solution[0], 'sec', axis=0, tiled=True)  6.5 us
    all_gather x1, blocking collectives, local(): around = lax.all_gather(packed, 'sec', axis=0)  6.37 us
    ppermute x3, starting transfers between devices, swap_by_section(): return lax.ppermute(array, ('sec', 'sub'), moves)  5.91 us
    all_gather x1, blocking collectives, local(): precond_all = lax.all_gather(precond, 'sec', axis=0, tiled=True)  5.78 us
    ppermute x6, waiting for transfers between devices, swap_columns(): lax.ppermute(array, 'sub', [(i, partner(kind, i, count)) for i in range(c...  4.73 us
    dot_general x10, matrix products, dot(): return jnp.dot(a, b, preferred_element_type=F32)  3.18 us
    ppermute x3, waiting for transfers between devices, swap_by_section(): return lax.ppermute(array, ('sec', 'sub'), moves)  2.13 us
  transfers between devices with their start and end apart: 10, of which 4 were waited for; matrix products, arithmetic and copies ran while one was open for 9% of the time, Pallas kernels for 0%

commit v1 on v0

--- a/solution.py
+++ b/solution.py
@@ -6,6 +6,16 @@
 F32 = jnp.float32
 BF16 = jnp.bfloat16
 KINDS = ("A2", "B2", "A3", "B3")
+
+
+def turned_line(value, mesh_axis, dim):
+    size = lax.axis_size(mesh_axis)
+    held, pieces = (value, [value])
+    for _ in range(size - 1):
+        held = lax.ppermute(held, mesh_axis, [(i, (i + 1) % size) for i in range(size)])
+        pieces.insert(0, held)
+    flat = jnp.concatenate(pieces, axis=dim)
+    return jnp.roll(flat, (lax.axis_index(mesh_axis) + 1) * value.shape[dim], axis=dim)
 
 
 def partner(kind, i, count):
@@ -188,7 +198,7 @@
     picked = dot(gather, coarse.reshape(unknowns, -1)).astype(BF16)
     facing = dot(selector, jnp.where(want_a, cor_a[:face_len], cor_b[:face_len]))
     precond = (0.5 * (correction + facing + dot(weights_pair, picked))).astype(BF16)
-    precond_all = lax.all_gather(precond, "sec", axis=0, tiled=True)
+    precond_all = turned_line(precond, "sec", 0)
     image = dot(s_rows, precond_all).astype(BF16)
     return (precond[None], image[None])
 

time: 52.2 us -> 57.7 us (1.11)
  waiting for transfers between devices: 6.86 us -> 17.9 us
  blocking collectives: 18.6 us -> 12.9 us
    ppermute x0 -> x3, waiting for transfers between devices: none -> 11.1 us  [turned_line(): lax.ppermute(held, mesh_axis, [(i, (i + 1) % size) for i in range(size)])]
    all_gather x1 -> x0, blocking collectives: 5.78 us -> none  [local(): precond_all = lax.all_gather(precond, 'sec', axis=0, tiled=True)]
  transfers between devices with their start and end apart: 10 -> 13, of which waited for: 4 -> 7; matrix products, arithmetic and copies ran while one was open for 9% -> 8% of each run, Pallas kernels for 0% -> 0%
where the time goes in v1:
time: 57.7 us; the launch traced here: 57.5 us
  waiting for transfers between devices  17.9 us (31%)
  starting transfers between devices  16.8 us (29%)
  blocking collectives  12.9 us (22%)
  matrix products  3.55 us (6%)
  other arithmetic  2.93 us (5%)
  between operations  1.81 us (3%)
  local copies, waits for them, and re-layouts  1.6 us (3%)
    ppermute x3, waiting for transfers between devices, turned_line(): lax.ppermute(held, mesh_axis, [(i, (i + 1) % size) for i in range(size)])  11.1 us
    ppermute x6, starting transfers between devices, swap_columns(): lax.ppermute(array, 'sub', [(i, partner(kind, i, count)) for i in range(c...  9.27 us
    all_gather x1, blocking collectives, local(): iterate = lax.all_gather(solution[0], 'sec', axis=0, tiled=True)  6.5 us
    all_gather x1, blocking collectives, local(): around = lax.all_gather(packed, 'sec', axis=0)  6.37 us
    ppermute x3, starting transfers between devices, swap_by_section(): return lax.ppermute(array, ('sec', 'sub'), moves)  5.91 us
    ppermute x6, waiting for transfers between devices, swap_columns(): lax.ppermute(array, 'sub', [(i, partner(kind, i, count)) for i in range(c...  4.73 us
    dot_general x10, matrix products, dot(): return jnp.dot(a, b, preferred_element_type=F32)  3.19 us
    ppermute x3, waiting for transfers between devices, swap_by_section(): return lax.ppermute(array, ('sec', 'sub'), moves)  2.13 us
  transfers between devices with their start and end apart: 13, of which 7 were waited for; matrix products, arithmetic and copies ran while one was open for 8% of the time, Pallas kernels for 0%

profile of v1, /device:TPU:0, one launch (start us, length us, event | category | flops | bytes accessed | tf_op | source)
XLA Modules:
  0.0 57.5 jit_solution(16660198952854463232)
XLA Ops:
  0.6 0.0 copy-start
  0.6 0.0 copy-start.5
  0.7 0.7 %fusion.86 = (bf16[1,128]{1,0:T(2,128)(2,1)S(1)}, s32[1,128]{1,0:T(1,128)S(1)}) fusion(s32[1,128]{1,0:T(1,128)} %param.17, s32[]{:T(128)S(6)} %axis_index.29), kind=kLoop, calls=%fused_computation.226 | loop fusion | flops 5504 | bytes 1284 | tf_op jit(solution)/shard_map/convert.3
  1.4 3.1 %collective-permute-start.4 = (bf16[16,128]{1,0:T(8,128)(2,1)S(1)}, bf16[16,128]{1,0:T(8,128)(2,1)S(1)}, u32[]{:S(2)}, u32[]{:S(2)}) collective-permute-start(bf16[16,128]{1,0:T(8,128)(2,1)S(1)} %pad.8), channel_id=1, source_target_pairs={{0,2},{1,3},{2,0},{3,1},{4,6},{5,7},{6,4},{7,5},{8,14},{9,15},{10,... | collective-permute-start | bytes 12296 | tf_op jit(solution)/shard_map/ppermute | solution.py:46
  4.6 0.8 %pad_maximum_fusion.2 = bf16[272,128]{1,0:T(8,128)(2,1)S(1)} fusion(bf16[16,128]{1,0:T(8,128)(2,1)S(1)} %pad.8, bf16[256,128]{1,0:T(8,128)(2,1)} %bitcast.261), kind=kLoop, calls=%fused_computation.55 | loop fusion | flops 139264 | bytes 139264 | tf_op jit(solution)/shard_map/concatenate | solution.py:97
  5.4 3.4 %collective-permute-start.3 = (bf16[272,128]{1,0:T(8,128)(2,1)S(1)}, bf16[272,128]{1,0:T(8,128)(2,1)S(1)}, u32[]{:S(2)}, u32[]{:S(2)}) collective-permute-start(bf16[272,128]{1,0:T(8,128)(2,1)S(1)} %pad_maximum_fusion.2), channel_id=1, source_target_pairs={{0,7},{1,2},{2,1},{3,4},{4,3},{5,6},{6,5},{7,0},{8,15},{9,10},{10,... | collective-permute-start | bytes 208904 | tf_op jit(solution)/shard_map/ppermute | solution.py:36
  8.8 0.0 collective-permute-start.2
  8.8 6.5 %all-gather = bf16[1,1024,128]{2,1,0:T(8,128)(2,1)S(1)} all-gather(bf16[1,256,128]{2,1,0:T(8,128)(2,1)} %param.13), channel_id=2, replica_groups=mesh['sec'=4,'sub'=8] {'sec'}, dimensions={1}, use_global_device_ids=true | all-gather | bytes 327680 | tf_op jit(solution)/shard_map/all_gather | solution.py:100
  15.3 0.0 copy-done
  15.3 0.0 copy-done.5
  15.3 0.0 copy-start.7
  15.4 0.0 copy-start.6
  15.4 0.0 copy-start.4
  15.4 0.3 fusion.97
  15.7 2.6 %collective-permute-start.1 = (bf16[256,128]{1,0:T(8,128)(2,1)S(1)}, bf16[256,128]{1,0:T(8,128)(2,1)S(1)}, u32[]{:S(2)}, u32[]{:S(2)}) collective-permute-start(bf16[256,128]{1,0:T(8,128)(2,1)S(1)} %get-tuple-element.63), channel_id=1, source_target_pairs={{0,7},{1,2},{2,1},{3,4},{4,3},{5,6},{6,5},{7,0},{8,15},{9,10},{10,... | collective-permute-start | bytes 196616 | tf_op jit(solution)/shard_map/ppermute | solution.py:36
  18.2 0.5 collective-permute-start
  18.9 0.0 copy-done.7
  18.9 0.6 %constant_dynamic-slice_fusion = s32[1,1]{1,0:T(1,128)} fusion(s32[1,4]{1,0:T(1,128)S(1)} %copy-done.7, s32[]{:T(128)S(6)} %select_n.309), kind=kLoop, calls=%fused_computation.191 | loop fusion | bytes 12 | tf_op jit(solution)/shard_map/dynamic_slice | solution.py:105
  20.1 0.0 copy-start.3
  20.2 2.7 %collective-permute-done.1 = bf16[256,128]{1,0:T(8,128)(2,1)S(1)} collective-permute-done((bf16[256,128]{1,0:T(8,128)(2,1)S(1)}, bf16[256,128]{1,0:T(8,128)(2,1)S(1)}, u32[]{:S(2)}, u32[]{:S(2)}) %collective-permute-start.1) | collective-permute-done | bytes 65568 | tf_op jit(solution)/shard_map/ppermute | solution.py:36
  22.9 0.8 %collective-permute-done = bf16[256,128]{1,0:T(8,128)(2,1)S(1)} collective-permute-done((bf16[256,128]{1,0:T(8,128)(2,1)S(1)}, bf16[256,128]{1,0:T(8,128)(2,1)S(1)}, u32[]{:S(2)}, u32[]{:S(2)}) %collective-permute-start) | collective-permute-done | bytes 65568 | tf_op jit(solution)/shard_map/ppermute | solution.py:36
  23.7 0.0 copy-done.6
  23.7 0.2 fusion.7
  24.0 0.0 copy-done.4
  24.0 0.2 fusion.10
  24.2 0.0 collective-permute-done.3
  24.2 0.0 collective-permute-done.2
  24.4 0.2 convert_reduce_fusion.1
  24.7 0.4 fusion.2
  25.1 0.0 copy-done.3
  25.1 0.4 fusion.11
  25.5 0.0 collective-permute-done.4
  25.5 6.4 %all-gather.1 = bf16[1856,128]{1,0:T(8,128)(2,1)S(1)} all-gather(bf16[464,128]{1,0:T(8,128)(2,1)S(1)} %fusion.32), channel_id=3, replica_groups=mesh['sec'=4,'sub'=8] {'sec'}, dimensions={0}, use_global_device_ids=true | all-gather | bytes 593920 | tf_op jit(solution)/shard_map/all_gather | solution.py:133
  31.9 0.0 copy-start.2
  32.0 1.0 %collective-permute-start.8 = (bf16[128,128]{1,0:T(8,128)(2,1)S(1)}, bf16[128,128]{1,0:T(8,128)(2,1)S(1)}, u32[]{:S(2)}, u32[]{:S(2)}) collective-permute-start(bf16[128,128]{1,0:T(8,128)(2,1)S(1)} %slice_reduce_fusion), channel_id=1, source_target_pairs={{0,3},{1,6},{2,5},{3,0},{4,7},{5,2},{6,1},{7,4},{8,13},{9,12},{10,... | collective-permute-start | bytes 98312 | tf_op jit(solution)/shard_map/ppermute | solution.py:46
  33.0 0.0 copy-done.2
  33.0 0.3 fusion.98
  33.3 2.7 %collective-permute-start.6 = (bf16[448,128]{1,0:T(8,128)(2,1)S(1)}, bf16[448,128]{1,0:T(8,128)(2,1)S(1)}, u32[]{:S(2)}, u32[]{:S(2)}) collective-permute-start(bf16[448,128]{1,0:T(8,128)(2,1)S(1)} %pad_maximum_fusion), channel_id=1, source_target_pairs={{0,7},{1,2},{2,1},{3,4},{4,3},{5,6},{6,5},{7,0},{8,15},{9,10},{10,... | collective-permute-start | bytes 344072 | tf_op jit(solution)/shard_map/ppermute | solution.py:36
  36.0 0.0 collective-permute-start.5
  36.1 0.7 %convert_reduce_fusion = s32[896]{0:T(1024)S(1)} fusion(s32[896]{0:T(1024)S(1)} %get-tuple-element.46, s32[896]{0:T(1024)S(1)} %get-tuple-element.45), kind=kLoop, calls=%fused_computation | loop fusion | flops 4013184 | bytes 10752 | tf_op jit(solution)/shard_map/reduce_sum | solution.py:160
  36.9 1.8 %collective-permute-start.7 = (bf16[192,128]{1,0:T(8,128)(2,1)S(1)}, bf16[192,128]{1,0:T(8,128)(2,1)S(1)}, u32[]{:S(2)}, u32[]{:S(2)}) collective-permute-start(bf16[192,128]{1,0:T(8,128)(2,1)S(1)} %pad_maximum_fusion.3), channel_id=1, source_target_pairs={{0,2},{1,3},{2,0},{3,1},{4,6},{5,7},{6,4},{7,5},{8,14},{9,15},{10,... | collective-permute-start | bytes 147464 | tf_op jit(solution)/shard_map/ppermute | solution.py:46
  38.6 0.2 convolution_convert_fusion.3
  38.9 0.0 collective-permute-done.8
  38.9 2.1 %collective-permute-done.7 = bf16[192,128]{1,0:T(8,128)(2,1)S(1)} collective-permute-done((bf16[192,128]{1,0:T(8,128)(2,1)S(1)}, bf16[192,128]{1,0:T(8,128)(2,1)S(1)}, u32[]{:S(2)}, u32[]{:S(2)}) %collective-permute-start.7) | collective-permute-done | bytes 49184 | tf_op jit(solution)/shard_map/ppermute | solution.py:46
  41.0 1.6 %collective-permute-start.9 = (bf16[320,128]{1,0:T(8,128)(2,1)S(1)}, bf16[320,128]{1,0:T(8,128)(2,1)S(1)}, u32[]{:S(2)}, u32[]{:S(2)}) collective-permute-start(bf16[320,128]{1,0:T(8,128)(2,1)S(1)} %pad_maximum_fusion.1), channel_id=1, source_target_pairs={{0,8},{8,0},{16,24},{24,16},{1,9},{9,1},{17,25},{25,17},{2,10},{10... | collective-permute-start | bytes 245768 | tf_op jit(solution)/shard_map/ppermute | solution.py:50
  42.6 1.2 %collective-permute-done.5 = bf16[448,128]{1,0:T(8,128)(2,1)S(1)} collective-permute-done((bf16[448,128]{1,0:T(8,128)(2,1)S(1)}, bf16[448,128]{1,0:T(8,128)(2,1)S(1)}, u32[]{:S(2)}, u32[]{:S(2)}) %collective-permute-start.5) | collective-permute-done | bytes 114720 | tf_op jit(solution)/shard_map/ppermute | solution.py:36
  43.8 0.0 collective-permute-done.6
  43.9 0.0 collective-permute-done.9
  43.9 0.3 fusion.5
  44.3 0.1 convolution_convert_fusion
  44.4 0.5 fusion.9
  44.9 0.2 fusion.6
  45.1 0.0 copy-start.1
  45.1 0.1 collective-permute-start.10
  45.2 3.7 %collective-permute-done.10 = bf16[256,128]{1,0:T(8,128)(2,1)S(1)} collective-permute-done((bf16[256,128]{1,0:T(8,128)(2,1)S(1)}, bf16[256,128]{1,0:T(8,128)(2,1)S(1)}, u32[]{:S(2)}, u32[]{:S(2)}) %collective-permute-start.10) | collective-permute-done | bytes 65568 | tf_op jit(solution)/shard_map/ppermute | solution.py:15
  48.9 0.0 collective-permute-start.11
  48.9 3.7 %collective-permute-done.11 = bf16[256,128]{1,0:T(8,128)(2,1)S(1)} collective-permute-done((bf16[256,128]{1,0:T(8,128)(2,1)S(1)}, bf16[256,128]{1,0:T(8,128)(2,1)S(1)}, u32[]{:S(2)}, u32[]{:S(2)}) %collective-permute-start.11) | collective-permute-done | bytes 65568 | tf_op jit(solution)/shard_map/ppermute | solution.py:15
  52.6 0.0 collective-permute-start.12
  52.6 3.7 %collective-permute-done.12 = bf16[256,128]{1,0:T(8,128)(2,1)S(1)} collective-permute-done((bf16[256,128]{1,0:T(8,128)(2,1)S(1)}, bf16[256,128]{1,0:T(8,128)(2,1)S(1)}, u32[]{:S(2)}, u32[]{:S(2)}) %collective-permute-start.12) | collective-permute-done | bytes 65568 | tf_op jit(solution)/shard_map/ppermute | solution.py:15
  56.4 0.0 copy-done.1
  56.4 0.3 fusion.8
  56.7 0.7 %copy.14 = bf16[1,256,128]{2,1,0:T(8,128)(2,1)} copy(bf16[1,256,128]{1,2,0:T(8,128)(2,1)S(1)} %fusion.8) | data formatting | bytes 131072
  (56 shorter events, 0.7 us)
Async XLA Ops:
  0.6 14.7 %copy-start = (bf16[1,256,1024]{2,1,0:T(8,128)(2,1)S(1)}, bf16[1,256,1024]{2,1,0:T(8,128)(2,1)}, u32[]{:S(2)}) copy-start(bf16[1,256,1024]{2,1,0:T(8,128)(2,1)} %param.9) | copy-start | bytes 1572868
  0.6 14.7 %copy-start.5 = (bf16[1,256,128]{2,1,0:T(8,128)(2,1)S(1)}, bf16[1,256,128]{2,1,0:T(8,128)(2,1)}, u32[]{:S(2)}) copy-start(bf16[1,256,128]{2,1,0:T(8,128)(2,1)} %param.14) | copy-start | bytes 196612
  1.4 24.0 %collective-permute-start.4 = (bf16[16,128]{1,0:T(8,128)(2,1)S(1)}, bf16[16,128]{1,0:T(8,128)(2,1)S(1)}, u32[]{:S(2)}, u32[]{:S(2)}) collective-permute-start(bf16[16,128]{1,0:T(8,128)(2,1)S(1)} %pad.8), channel_id=1, source_target_pairs={{0,2},{1,3},{2,0},{3,1},{4,6},{5,7},{6,4},{7,5},{8,14},{9,15},{10,... | collective-permute-start | bytes 12296 | tf_op jit(solution)/shard_map/ppermute | solution.py:46
  5.4 18.8 %collective-permute-start.3 = (bf16[272,128]{1,0:T(8,128)(2,1)S(1)}, bf16[272,128]{1,0:T(8,128)(2,1)S(1)}, u32[]{:S(2)}, u32[]{:S(2)}) collective-permute-start(bf16[272,128]{1,0:T(8,128)(2,1)S(1)} %pad_maximum_fusion.2), channel_id=1, source_target_pairs={{0,7},{1,2},{2,1},{3,4},{4,3},{5,6},{6,5},{7,0},{8,15},{9,10},{10,... | collective-permute-start | bytes 208904 | tf_op jit(solution)/shard_map/ppermute | solution.py:36
  8.8 15.4 %collective-permute-start.2 = (bf16[272,128]{1,0:T(8,128)(2,1)S(1)}, bf16[272,128]{1,0:T(8,128)(2,1)S(1)}, u32[]{:S(2)}, u32[]{:S(2)}) collective-permute-start(bf16[272,128]{1,0:T(8,128)(2,1)S(1)} %pad_maximum_fusion.2), channel_id=1, source_target_pairs={{0,1},{1,0},{2,3},{3,2},{4,5},{5,4},{6,7},{7,6},{8,9},{9,8},{10,11... | collective-permute-start | bytes 208904 | tf_op jit(solution)/shard_map/ppermute | solution.py:36
  15.3 3.5 %copy-start.7 = (s32[1,4]{1,0:T(1,128)S(1)}, s32[1,4]{1,0:T(1,128)}, u32[]{:S(2)}) copy-start(s32[1,4]{1,0:T(1,128)} %param.15) | copy-start | bytes 52
  15.4 8.4 %copy-start.6 = (s32[1,256]{1,0:T(1,128)S(1)}, s32[1,256]{1,0:T(1,128)}, u32[]{:S(2)}) copy-start(s32[1,256]{1,0:T(1,128)} %param.16) | copy-start | bytes 3076
  15.4 8.6 %copy-start.4 = (bf16[1,256,128]{2,1,0:T(8,128)(2,1)S(1)}, bf16[1,256,128]{2,1,0:T(8,128)(2,1)}, u32[]{:S(2)}) copy-start(bf16[1,256,128]{2,1,0:T(8,128)(2,1)} %param.11) | copy-start | bytes 196612
  15.7 7.2 %collective-permute-start.1 = (bf16[256,128]{1,0:T(8,128)(2,1)S(1)}, bf16[256,128]{1,0:T(8,128)(2,1)S(1)}, u32[]{:S(2)}, u32[]{:S(2)}) collective-permute-start(bf16[256,128]{1,0:T(8,128)(2,1)S(1)} %get-tuple-element.63), channel_id=1, source_target_pairs={{0,7},{1,2},{2,1},{3,4},{4,3},{5,6},{6,5},{7,0},{8,15},{9,10},{10,... | collective-permute-start | bytes 196616 | tf_op jit(solution)/shard_map/ppermute | solution.py:36
  18.2 5.5 %collective-permute-start = (bf16[256,128]{1,0:T(8,128)(2,1)S(1)}, bf16[256,128]{1,0:T(8,128)(2,1)S(1)}, u32[]{:S(2)}, u32[]{:S(2)}) collective-permute-start(bf16[256,128]{1,0:T(8,128)(2,1)S(1)} %get-tuple-element.63), channel_id=1, source_target_pairs={{0,1},{1,0},{2,3},{3,2},{4,5},{5,4},{6,7},{7,6},{8,9},{9,8},{10,11... | collective-permute-start | bytes 196616 | tf_op jit(solution)/shard_map/ppermute | solution.py:36
  20.1 4.9 %copy-start.3 = (bf16[1,192,768]{2,1,0:T(8,128)(2,1)S(1)}, bf16[1,192,768]{2,1,0:T(8,128)(2,1)}, u32[]{:S(2)}) copy-start(bf16[1,192,768]{2,1,0:T(8,128)(2,1)} %param.12) | copy-start | bytes 884740
  31.9 1.1 %copy-start.2 = (bf16[1,256,1024]{2,1,0:T(8,128)(2,1)S(1)}, bf16[1,256,1024]{2,1,0:T(8,128)(2,1)}, u32[]{:S(2)}) copy-start(bf16[1,256,1024]{2,1,0:T(8,128)(2,1)} %param.10) | copy-start | bytes 1572868
  32.0 7.0 %collective-permute-start.8 = (bf16[128,128]{1,0:T(8,128)(2,1)S(1)}, bf16[128,128]{1,0:T(8,128)(2,1)S(1)}, u32[]{:S(2)}, u32[]{:S(2)}) collective-permute-start(bf16[128,128]{1,0:T(8,128)(2,1)S(1)} %slice_reduce_fusion), channel_id=1, source_target_pairs={{0,3},{1,6},{2,5},{3,0},{4,7},{5,2},{6,1},{7,4},{8,13},{9,12},{10,... | collective-permute-start | bytes 98312 | tf_op jit(solution)/shard_map/ppermute | solution.py:46
  33.3 10.5 %collective-permute-start.6 = (bf16[448,128]{1,0:T(8,128)(2,1)S(1)}, bf16[448,128]{1,0:T(8,128)(2,1)S(1)}, u32[]{:S(2)}, u32[]{:S(2)}) collective-permute-start(bf16[448,128]{1,0:T(8,128)(2,1)S(1)} %pad_maximum_fusion), channel_id=1, source_target_pairs={{0,7},{1,2},{2,1},{3,4},{4,3},{5,6},{6,5},{7,0},{8,15},{9,10},{10,... | collective-permute-start | bytes 344072 | tf_op jit(solution)/shard_map/ppermute | solution.py:36
  36.0 7.8 %collective-permute-start.5 = (bf16[448,128]{1,0:T(8,128)(2,1)S(1)}, bf16[448,128]{1,0:T(8,128)(2,1)S(1)}, u32[]{:S(2)}, u32[]{:S(2)}) collective-permute-start(bf16[448,128]{1,0:T(8,128)(2,1)S(1)} %pad_maximum_fusion), channel_id=1, source_target_pairs={{0,1},{1,0},{2,3},{3,2},{4,5},{5,4},{6,7},{7,6},{8,9},{9,8},{10,11... | collective-permute-start | bytes 344072 | tf_op jit(solution)/shard_map/ppermute | solution.py:36
  36.9 4.2 %collective-permute-start.7 = (bf16[192,128]{1,0:T(8,128)(2,1)S(1)}, bf16[192,128]{1,0:T(8,128)(2,1)S(1)}, u32[]{:S(2)}, u32[]{:S(2)}) collective-permute-start(bf16[192,128]{1,0:T(8,128)(2,1)S(1)} %pad_maximum_fusion.3), channel_id=1, source_target_pairs={{0,2},{1,3},{2,0},{3,1},{4,6},{5,7},{6,4},{7,5},{8,14},{9,15},{10,... | collective-permute-start | bytes 147464 | tf_op jit(solution)/shard_map/ppermute | solution.py:46
  41.0 2.8 %collective-permute-start.9 = (bf16[320,128]{1,0:T(8,128)(2,1)S(1)}, bf16[320,128]{1,0:T(8,128)(2,1)S(1)}, u32[]{:S(2)}, u32[]{:S(2)}) collective-permute-start(bf16[320,128]{1,0:T(8,128)(2,1)S(1)} %pad_maximum_fusion.1), channel_id=1, source_target_pairs={{0,8},{8,0},{16,24},{24,16},{1,9},{9,1},{17,25},{25,17},{2,10},{10... | collective-permute-start | bytes 245768 | tf_op jit(solution)/shard_map/ppermute | solution.py:50
  45.1 11.3 %copy-start.1 = (bf16[256,128]{1,0:T(8,128)(2,1)}, bf16[256,128]{1,0:T(8,128)(2,1)S(1)}, u32[]{:S(2)}) copy-start(bf16[256,128]{1,0:T(8,128)(2,1)S(1)} %fusion.6) | copy-start | bytes 196612
  45.1 3.7 %collective-permute-start.10 = (bf16[256,128]{1,0:T(8,128)(2,1)S(1)}, bf16[256,128]{1,0:T(8,128)(2,1)S(1)}, u32[]{:S(2)}, u32[]{:S(2)}) collective-permute-start(bf16[256,128]{1,0:T(8,128)(2,1)S(1)} %fusion.6), channel_id=1, source_target_pairs={{0,8},{8,16},{16,24},{24,0},{1,9},{9,17},{17,25},{25,1},{2,10},{10... | collective-permute-start | bytes 196616 | tf_op jit(solution)/shard_map/ppermute | solution.py:15
  48.9 3.7 %collective-permute-start.11 = (bf16[256,128]{1,0:T(8,128)(2,1)S(1)}, bf16[256,128]{1,0:T(8,128)(2,1)S(1)}, u32[]{:S(2)}, u32[]{:S(2)}) collective-permute-start(bf16[256,128]{1,0:T(8,128)(2,1)S(1)} %collective-permute-done.10), channel_id=1, source_target_pairs={{0,8},{8,16},{16,24},{24,0},{1,9},{9,17},{17,25},{25,1},{2,10},{10... | collective-permute-start | bytes 196616 | tf_op jit(solution)/shard_map/ppermute | solution.py:15
  52.6 3.7 %collective-permute-start.12 = (bf16[256,128]{1,0:T(8,128)(2,1)S(1)}, bf16[256,128]{1,0:T(8,128)(2,1)S(1)}, u32[]{:S(2)}, u32[]{:S(2)}) collective-permute-start(bf16[256,128]{1,0:T(8,128)(2,1)S(1)} %collective-permute-done.11), channel_id=1, source_target_pairs={{0,8},{8,16},{16,24},{24,0},{1,9},{9,17},{17,25},{25,1},{2,10},{10... | collective-permute-start | bytes 196616 | tf_op jit(solution)/shard_map/ppermute | solution.py:15
